TPU v7x, 32 devices: a whole 2x2x4 slice. The times are simulated.
32 devices in a mesh: top: 4 (over x, core), mid: 2 (over y), leaf: 4 (over z).
Axes of the slice: x: 2, y: 2, z: 4, core: 2. Of those that a mesh axis runs over, the one named last changes fastest.
Arguments:
- rhs: bfloat16 [49152, 256], P(('top', 'mid', 'leaf')), may hold values from -6 to 6
- guess: bfloat16 [49152, 256], P(('top', 'mid', 'leaf')), may hold values from -3 to 3
- diag_blocks: bfloat16 [32, 1536, 1536], P(('top', 'mid', 'leaf')), as said below
- precond: bfloat16 [32, 1536, 1536], P(('top', 'mid', 'leaf'))
- bases: bfloat16 [32, 1536, 128], P(('top', 'mid', 'leaf')), may hold values from -0.3125 to 0.3125
- leaf_to_middle_transfer: bfloat16 [32, 128, 128], P(('top', 'mid', 'leaf')), may hold values from -0.25 to 0.25
- mid_transfer: bfloat16 [8, 128, 128], replicated, may hold values from -0.375 to 0.375
- leaf_coupling: bfloat16 [32, 4, 128, 128], P(('top', 'mid', 'leaf')), may hold values from -0.25 to 0.25
- cluster_coupling: bfloat16 [8, 3, 128, 128], P(('top', 'mid')), may hold values from -0.3125 to 0.3125
- group_coupling: bfloat16 [4, 2, 128, 128], P('top'), may hold values from -0.375 to 0.375
- leaf_lists: int32 [32, 4], P(('top', 'mid', 'leaf')), may hold values from 0 to 3, as said below
- owner: int32 [8, 4], P(('top', 'mid')), may hold values from 0 to 3, as said below
- cluster_lists: int32 [8, 3], P(('top', 'mid')), may hold values from 0 to 7, as said below
- group_lists: int32 [4, 2], P('top'), may hold values from 0 to 3, as said below
Outputs:
- solution: bfloat16 [49152, 256], P(('top', 'mid', 'leaf'))
Inputs may be any that keep to these rules, and one draw needn't show every extreme that they name: `leaf_lists`: each row holds 4 distinct sibling cluster ids. `owner`: each row is a permutation of the slots of the cluster. `cluster_lists`: each row holds 3 distinct cluster ids. `group_lists`: each row holds 2 distinct group ids. `diag_blocks`: each block is a diagonal with entries from 1 to 3 plus small dense noise.
All inputs are finite; a program needn't handle non-finite values.
Results may differ from a plain program's by a relative error of at most 0.028.
Values may be sent and summed in bfloat16 or wider, within the bound.
No kernel may reach another device: no remote copies, remote signals or barrier semaphores. Data moves between devices by JAX's collectives and lax.ppermute only.
A program may use at most 64 MiB of HBM per device.

v0:
```python
import jax
import jax.numpy as jnp
from jax import lax
from jax.sharding import PartitionSpec as P

damping = 0.7


def far_field(
    vector,
    bases,
    leaf_to_middle_transfer,
    mid_transfer,
    leaf_coupling,
    cluster_coupling,
    group_coupling,
    slots,
    cluster_lists,
    group_lists,
):
    single_precision = jnp.float32
    brain_float_sixteen = jnp.bfloat16
    rank = bases.shape[2]
    columns = vector.shape[1]
    leaf_coefficient = jnp.einsum(
        "na,nr->ar", bases[0], vector, preferred_element_type=single_precision
    ).astype(brain_float_sixteen)
    upward_contribution = jnp.einsum(
        "ba,br->ar",
        leaf_to_middle_transfer[0],
        leaf_coefficient,
        preferred_element_type=single_precision,
    ).astype(brain_float_sixteen)
    sibling_coefs = lax.all_gather(leaf_coefficient, "leaf", axis=0, tiled=True).reshape(
        -1, rank, columns
    )
    cluster_coef = lax.psum(
        upward_contribution.astype(single_precision).astype(jnp.bfloat16), "leaf"
    ).astype(jnp.float32)
    cluster_half = cluster_coef.astype(brain_float_sixteen)
    cluster_index = lax.axis_index(("top", "mid"))
    own_transfer = lax.dynamic_index_in_dim(mid_transfer, cluster_index, 0, keepdims=False)
    all_clusters = lax.all_gather(cluster_half, ("top", "mid"), axis=0, tiled=True).reshape(
        -1, rank, columns
    )
    group_terms = jnp.einsum(
        "cba,cbr->car", mid_transfer, all_clusters, preferred_element_type=single_precision
    )
    group_coefs = jnp.sum(
        group_terms.reshape(-1, lax.axis_size("mid"), rank, columns), axis=1
    ).astype(brain_float_sixteen)
    group_far = jnp.einsum(
        "kab,kbr->ar",
        group_coupling[0],
        jnp.take(group_coefs, group_lists[0], axis=0),
        preferred_element_type=single_precision,
    )
    cluster_far = jnp.einsum(
        "kab,kbr->ar",
        cluster_coupling[0],
        jnp.take(all_clusters, cluster_lists[0], axis=0),
        preferred_element_type=single_precision,
    )
    picked = jnp.take(sibling_coefs, slots, axis=0)
    leaf_distant_field = jnp.einsum(
        "kab,kbr->ar", leaf_coupling[0], picked, preferred_element_type=single_precision
    )
    cluster_total = (
        cluster_far
        + jnp.dot(
            own_transfer,
            group_far.astype(brain_float_sixteen),
            preferred_element_type=single_precision,
        )
    ).astype(brain_float_sixteen)
    leaf_grand_total = (
        leaf_distant_field
        + jnp.dot(
            leaf_to_middle_transfer[0], cluster_total, preferred_element_type=single_precision
        )
    ).astype(brain_float_sixteen)
    return jnp.dot(bases[0], leaf_grand_total, preferred_element_type=single_precision)


def body(
    rhs,
    guess,
    diag_blocks,
    precond,
    bases,
    leaf_to_middle_transfer,
    mid_transfer,
    leaf_coupling,
    cluster_coupling,
    group_coupling,
    leaf_lists,
    owner,
    cluster_lists,
    group_lists,
):
    slots = jnp.take(owner[0], leaf_lists[0], axis=0)

    def apply_matrix(vector):
        near_part = jnp.dot(diag_blocks[0], vector, preferred_element_type=jnp.float32)
        return near_part + far_field(
            vector,
            bases,
            leaf_to_middle_transfer,
            mid_transfer,
            leaf_coupling,
            cluster_coupling,
            group_coupling,
            slots,
            cluster_lists,
            group_lists,
        )

    def smooth(residual):
        return jnp.dot(
            precond[0], residual.astype(jnp.bfloat16), preferred_element_type=jnp.float32
        )

    target = rhs.astype(jnp.float32)
    residual = target - apply_matrix(guess)
    first = guess.astype(jnp.float32) + damping * smooth(residual)
    residual = target - apply_matrix(first.astype(jnp.bfloat16))
    second = first + damping * smooth(residual)
    return second.astype(jnp.bfloat16)


def solution(mesh):
    in_specs = (
        P(("top", "mid", "leaf"), None),
        P(("top", "mid", "leaf"), None),
        P(("top", "mid", "leaf"), None, None),
        P(("top", "mid", "leaf"), None, None),
        P(("top", "mid", "leaf"), None, None),
        P(("top", "mid", "leaf"), None, None),
        P(),
        P(("top", "mid", "leaf"), None, None, None),
        P(("top", "mid"), None, None, None),
        P("top", None, None, None),
        P(("top", "mid", "leaf"), None),
        P(("top", "mid"), None),
        P(("top", "mid"), None),
        P("top", None),
    )
    out_specs = P(("top", "mid", "leaf"), None)
    return jax.shard_map(body, mesh=mesh, in_specs=in_specs, out_specs=out_specs, check_vma=False)
```

profile of v0, /device:TPU:1, one launch (start us, length us, event | category | flops | bytes accessed | tf_op | source)
XLA Modules:
  0.0 158.7 jit_solution(18310039830741658121)
XLA Ops:
  6.5 0.0 copy-start
  6.5 0.0 all-reduce.3.cloned.1.call-start
  6.6 0.9 copy-done
  7.5 1.5 convolution_convert_fusion.1
  9.0 1.6 fusion.41
  10.6 0.0 all-reduce.3.cloned.1.call-update
  10.6 0.0 all-reduce.5.cloned.1.call-start
  10.7 1.3 compare_and_fusion.1
  11.9 0.7 compare_select_fusion.1
  12.6 0.7 compare_and_fusion
  13.2 0.7 compare_select_fusion
  13.9 13.3 %all_gather.12 = bf16[512,256]{1,0:T(8,128)(2,1)S(1)} all-gather(bf16[128,256]{1,0:T(8,128)(2,1)S(1)} %convolution_convert_fusion.1), channel_id=1, replica_groups=mesh['top'=4,'mid'=2,'leaf'=4] {'leaf'}, dimensions={0}, use_global_device_ids=true | all-gather | bytes 327680 | tf_op jit(solution)/shard_map/all_gather | solution.py:34
  27.2 0.0 copy-done.3
  27.2 1.1 copy.41
  28.4 0.0 copy-done.9
  28.4 0.0 copy-done.1
  28.4 0.6 gather_fusion
  29.1 0.0 copy-start.10
  29.1 0.0 copy-start.12
  29.1 4.9 %fusion.6 = f32[1536,256]{1,0:T(8,128)} fusion(bf16[1536,256]{1,0:T(8,128)(2,1)S(1)} %copy-done.3, bf16[1,1536,1536]{2,1,0:T(8,128)(2,1)} %param.22), kind=kOutput, calls=%fused_computation.13 | convolution fusion | flops 1207959552 | bytes 7077888 | tf_op jit(solution)/shard_map/dot_general | solution.py:104
  34.0 0.6 gather_fusion.1
  34.6 0.0 copy-done.10
  34.6 0.0 copy-done.12
  34.6 1.0 convolution_bitcast_fusion.2
  35.6 9.6 %all-reduce.3.cloned.1.call-done = bf16[128,256]{0,1:T(8,128)(2,1)} async-done(((bf16[128,256]{0,1:T(8,128)(2,1)}), bf16[128,256]{0,1:T(8,128)(2,1)}) %all-reduce.3.cloned.1.call-update) | async-done | bytes 65552 | tf_op jit(solution)/shard_map/psum | solution.py:37
  45.2 20.7 %all_gather.13 = bf16[1024,256]{0,1:T(8,128)(2,1)S(1)} all-gather(bf16[128,256]{0,1:T(8,128)(2,1)} %all-reduce.3.cloned.1.call-done), channel_id=1, replica_groups=mesh['top'=4,'mid'=2,'leaf'=4] {'top','mid'}, dimensions={0}, use_global_device_ids=true | all-gather | bytes 589824 | tf_op jit(solution)/shard_map/all_gather | solution.py:43
  65.9 0.2 copy.67
  66.1 0.0 copy-start.5
  66.1 1.3 gather_fusion.2
  67.3 0.0 copy-done.7
  67.3 1.1 bitcast_reduce_fusion.1
  68.4 1.5 gather_fusion.3
  69.9 1.3 convolution_bitcast_fusion.6
  71.2 1.2 fusion.37
  72.5 0.0 copy-done.2
  72.5 0.0 copy-done.5
  72.5 2.4 %fusion.33 = bf16[1536,256]{1,0:T(8,128)(2,1)} fusion(f32[1536,256]{1,0:T(8,128)S(1)} %copy-done.5, bf16[1536,256]{1,0:T(8,128)(2,1)S(1)} %copy-done.2, f32[256,128]{1,0:T(8,128)} %convolution_bitcast_fusion.2, bf16[128,256]{0,1:T(8,128)(2,1)S(1)} %fusion.37, bf16[1,1536,128]{2,1,0:T(8,128)(2,1)S(1)} %copy-done, bf16[1,128,128]{2,1,0:T(8,128)(2,1)} %param.25), kind=kOutput, calls=%fused_computation.28 | convolution fusion | flops 110690304 | bytes 3768320 | tf_op jit(solution)/shard_map/dot_general | solution.py:82
  74.8 4.2 %fusion.24 = f32[1536,256]{0,1:T(8,128)S(1)} fusion(bf16[1536,256]{1,0:T(8,128)(2,1)} %fusion.33, bf16[1,1536,1536]{2,1,0:T(8,128)(2,1)} %param.23, bf16[1536,256]{0,1:T(8,128)(2,1)} %copy.41), kind=kOutput, calls=%fused_computation.25 | convolution fusion | flops 1209139200 | bytes 7864320 | tf_op jit(solution)/shard_map/dot_general | solution.py:119
  79.1 0.0 copy-start.6
  79.1 0.4 convolution_convert_fusion
  79.4 0.0 copy-start.8
  79.4 5.1 %fusion.4 = f32[256,1536]{0,1:T(8,128)} fusion(bf16[1,1536,1536]{2,1,0:T(8,128)(2,1)} %param.22, f32[1536,256]{0,1:T(8,128)S(1)} %fusion.24), kind=kOutput, calls=%fused_computation.11 | convolution fusion | flops 1208352768 | bytes 7864320 | tf_op jit(solution)/shard_map/dot_general | solution.py:104
  84.6 0.0 copy-done.6
  84.6 0.0 copy-done.8
  84.6 0.8 fusion.42
  85.4 0.0 all-reduce.5.cloned.1.call-update
  85.4 11.6 %all_gather.14 = bf16[512,256]{0,1:T(8,128)(2,1)S(1)} all-gather(bf16[128,256]{0,1:T(8,128)(2,1)S(1)} %bitcast.168), channel_id=1, replica_groups=mesh['top'=4,'mid'=2,'leaf'=4] {'leaf'}, dimensions={0}, use_global_device_ids=true | all-gather | bytes 327680 | tf_op jit(solution)/shard_map/all_gather | solution.py:34
  97.0 0.1 copy.66
  97.1 0.6 gather_fusion.4
  97.7 0.0 copy-done.11
  97.7 0.0 copy-done.13
  97.7 1.0 convolution_bitcast_fusion.1
  98.7 17.8 %all-reduce.5.cloned.1.call-done = bf16[128,256]{0,1:T(8,128)(2,1)} async-done(((bf16[128,256]{0,1:T(8,128)(2,1)}), bf16[128,256]{0,1:T(8,128)(2,1)}) %all-reduce.5.cloned.1.call-update) | async-done | bytes 65552 | tf_op jit(solution)/shard_map/psum | solution.py:37
  116.5 20.7 %all_gather.15 = bf16[1024,256]{0,1:T(8,128)(2,1)S(1)} all-gather(bf16[128,256]{0,1:T(8,128)(2,1)} %all-reduce.5.cloned.1.call-done), channel_id=1, replica_groups=mesh['top'=4,'mid'=2,'leaf'=4] {'top','mid'}, dimensions={0}, use_global_device_ids=true | all-gather | bytes 589824 | tf_op jit(solution)/shard_map/all_gather | solution.py:43
  137.2 0.2 copy.68
  137.4 0.0 copy-start.4
  137.4 1.2 gather_fusion.5
  138.7 1.1 bitcast_reduce_fusion
  139.7 1.5 gather_fusion.6
  141.3 1.3 convolution_bitcast_fusion.4
  142.6 1.2 fusion.39
  143.8 2.4 %fusion.34 = bf16[1536,256]{1,0:T(8,128)(2,1)} fusion(f32[256,1536]{0,1:T(8,128)S(1)} %copy-done.4, bf16[1536,256]{1,0:T(8,128)(2,1)S(1)} %copy-done.2, f32[256,128]{1,0:T(8,128)} %convolution_bitcast_fusion.1, bf16[128,256]{0,1:T(8,128)(2,1)S(1)} %fusion.39, bf16[1,1536,128]{2,1,0:T(8,128)(2,1)S(1)} %copy-done, bf16[1,128,128]{2,1,0:T(8,128)(2,1)} %param.25), kind=kOutput, calls=%fused_computation.29 | convolution fusion | flops 110690304 | bytes 3768320 | tf_op jit(solution)/shard_map/dot_general | solution.py:82
  146.2 4.5 %fusion.30 = bf16[1536,256]{0,1:T(8,128)(2,1)S(1)} fusion(f32[1536,256]{0,1:T(8,128)} %copy-done.6, bf16[1536,256]{1,0:T(8,128)(2,1)} %fusion.34, bf16[1,1536,1536]{2,1,0:T(8,128)(2,1)} %param.23), kind=kOutput, calls=%fused_computation.27 | convolution fusion | flops 1209139200 | bytes 7864320 | tf_op jit(solution)/shard_map/dot_general | solution.py:119
  150.7 1.2 copy.56
  (16 shorter events, 0.1 us)
Async XLA Ops:
  6.5 1.0 copy-start
  6.5 20.7 %copy-start.3 = (bf16[1536,256]{1,0:T(8,128)(2,1)S(1)}, bf16[1536,256]{1,0:T(8,128)(2,1)}, u32[]{:S(2)}) copy-start(bf16[1536,256]{1,0:T(8,128)(2,1)} %param.21) | copy-start | bytes 2359300
  6.5 21.8 %copy-start.9 = (s32[1,4]{1,0:T(1,128)S(1)}, s32[1,4]{1,0:T(1,128)}, u32[]{:S(2)}) copy-start(s32[1,4]{1,0:T(1,128)} %param.30) | copy-start | bytes 52
  6.5 21.9 %copy-start.1 = (s32[1,4]{1,0:T(1,128)S(1)}, s32[1,4]{1,0:T(1,128)}, u32[]{:S(2)}) copy-start(s32[1,4]{1,0:T(1,128)} %param.31) | copy-start | bytes 52
  6.5 38.6 %all-reduce.3.cloned.1.call-start = ((), (), s32[]{:S(2)}) async-start(), calls=%async_computation | async-start | bytes 131072 | tf_op jit(solution)/shard_map/psum | solution.py:37
  10.6 105.9 %all-reduce.5.cloned.1.call-start = ((), (), s32[]{:S(2)}) async-start(), calls=%async_computation.1 | async-start | bytes 131072 | tf_op jit(solution)/shard_map/psum | solution.py:37
  29.1 5.5 %copy-start.10 = (pred[4]{0:T(512)(128)(4,1)}, pred[4]{0:T(512)(128)(4,1)S(1)}, u32[]{:S(2)}) copy-start(pred[4]{0:T(512)(128)(4,1)S(1)} %get-tuple-element.6) | copy-start | bytes 16
  29.1 5.5 %copy-start.12 = (bf16[1,4,128,128]{3,2,1,0:T(8,128)(2,1)S(1)}, bf16[1,4,128,128]{3,2,1,0:T(8,128)(2,1)}, u32[]{:S(2)}) copy-start(bf16[1,4,128,128]{3,2,1,0:T(8,128)(2,1)} %param.27) | copy-start | bytes 393220
  34.0 33.3 %copy-start.7 = (bf16[8,128,128]{2,1,0:T(8,128)(2,1)S(1)}, bf16[8,128,128]{2,1,0:T(8,128)(2,1)}, u32[]{:S(2)}) copy-start(bf16[8,128,128]{2,1,0:T(8,128)(2,1)} %param.26) | copy-start | bytes 786436
  65.9 6.6 %copy-start.2 = (bf16[1536,256]{1,0:T(8,128)(2,1)S(1)}, bf16[1536,256]{1,0:T(8,128)(2,1)}, u32[]{:S(2)}) copy-start(bf16[1536,256]{1,0:T(8,128)(2,1)} %param.20) | copy-start | bytes 2359300
  66.1 6.4 %copy-start.5 = (f32[1536,256]{1,0:T(8,128)S(1)}, f32[1536,256]{1,0:T(8,128)}, u32[]{:S(2)}) copy-start(f32[1536,256]{1,0:T(8,128)} %fusion.6) | copy-start | bytes 4718596
  79.1 5.5 %copy-start.6 = (f32[1536,256]{0,1:T(8,128)}, f32[1536,256]{0,1:T(8,128)S(1)}, u32[]{:S(2)}) copy-start(f32[1536,256]{0,1:T(8,128)S(1)} %fusion.24) | copy-start | bytes 4718596
  79.4 5.1 %copy-start.8 = (bf16[1,128,128]{2,1,0:T(8,128)(2,1)S(1)}, bf16[1,128,128]{2,1,0:T(8,128)(2,1)}, u32[]{:S(2)}) copy-start(bf16[1,128,128]{2,1,0:T(8,128)(2,1)} %param.25) | copy-start | bytes 98308
  84.6 13.1 %copy-start.11 = (pred[4]{0:T(512)(128)(4,1)S(1)}, pred[4]{0:T(512)(128)(4,1)}, u32[]{:S(2)}) copy-start(pred[4]{0:T(512)(128)(4,1)} %copy-done.10) | copy-start | bytes 16
  84.6 13.2 %copy-start.13 = (bf16[1,4,128,128]{3,2,1,0:T(8,128)(2,1)S(1)}, bf16[1,4,128,128]{3,2,1,0:T(8,128)(2,1)}, u32[]{:S(2)}) copy-start(bf16[1,4,128,128]{3,2,1,0:T(8,128)(2,1)} %param.27) | copy-start | bytes 393220
  98.7 42.6 %copy-start.14 = (pred[3]{0:T(512)(128)(4,1)S(1)}, pred[3]{0:T(512)(128)(4,1)}, u32[]{:S(2)}) copy-start(pred[3]{0:T(512)(128)(4,1)} %compare_and_fusion.1) | copy-start | bytes 13
  137.4 6.4 %copy-start.4 = (f32[256,1536]{0,1:T(8,128)S(1)}, f32[256,1536]{0,1:T(8,128)}, u32[]{:S(2)}) copy-start(f32[256,1536]{0,1:T(8,128)} %fusion.4) | copy-start | bytes 4718596
Sparse Core Ops, SparseCore 0:
  10.7 34.4 all-reduce.2
  85.5 31.0 all-reduce.4
where the time goes:
time: 159 us
  blocking collectives  66.3 us (42%)
  matrix products  36.8 us (23%)
  waiting for transfers between devices  27.4 us (17%)
  between operations  13.7 us (9%)
  local copies, waits for them, and re-layouts  11.1 us (7%)
  other arithmetic  3.27 us (2%)
    all_gather x2, blocking collectives, far_field(): lax.all_gather(cluster_half, ('top', 'mid'), axis=0, tiled=True)  41.3 us
    psum x2, waiting for transfers between devices, far_field(): lax.psum(upward_contribution.astype(single_precision).astype(jnp.bfloat16...  27.4 us
    all_gather x2, blocking collectives, far_field(): lax.all_gather(leaf_coefficient, 'leaf', axis=0, tiled=True)  25 us
    dot_general x2, matrix products, apply_matrix(): jnp.dot(diag_blocks[0], vector, preferred_element_type=jnp.float32)  10 us
    dot_general x2, matrix products, smooth(): jnp.dot(precond[0], residual.astype(jnp.bfloat16), preferred_element_type...  8.73 us
    dot_general x2, matrix products, far_field(): jnp.dot(bases[0], leaf_grand_total, preferred_element_type=single_precision)  4.72 us
  transfers between devices with their start and end apart: 2, of which 2 were waited for; matrix products, arithmetic and copies ran while one was open for 8% of the time, Pallas kernels for 0%

commit v1 on v0

--- a/solution.py
+++ b/solution.py
@@ -4,6 +4,12 @@
 from jax.sharding import PartitionSpec as P
 
 damping = 0.7
+
+
+def summed_here(array, axis):
+    parts = lax.all_gather(array, axis, axis=0, tiled=False)
+    total = parts.sum(axis=0)
+    return total
 
 
 def far_field(
@@ -34,7 +40,7 @@
     sibling_coefs = lax.all_gather(leaf_coefficient, "leaf", axis=0, tiled=True).reshape(
         -1, rank, columns
     )
-    cluster_coef = lax.psum(
+    cluster_coef = summed_here(
         upward_contribution.astype(single_precision).astype(jnp.bfloat16), "leaf"
     ).astype(jnp.float32)
     cluster_half = cluster_coef.astype(brain_float_sixteen)

time: 159 us -> 132 us (0.83)
  waiting for transfers between devices: 27.4 us -> 0 us
  blocking collectives: 66.3 us -> 90.3 us
  between operations: 13.7 us -> 0.38 us
  matrix products: 36.8 us -> 26.8 us
  local copies, waits for them, and re-layouts: 11.1 us -> 9.25 us
    psum x2 -> x0, waiting for transfers between devices: 27.4 us -> none  [far_field(): lax.psum(upward_contribution.astype(single_precision).astype(jnp.bfloat16...]
    all_gather x0 -> x2, blocking collectives: none -> 21.1 us  [summed_here(): parts = lax.all_gather(array, axis, axis=0, tiled=False)]
    all_gather x2, blocking collectives: 41.3 us -> 44.6 us  [far_field(): lax.all_gather(cluster_half, ('top', 'mid'), axis=0, tiled=True)]
    dot_general x2, matrix products: 2.37 us -> 0.33 us  [far_field(): jnp.einsum('ba,br->ar', leaf_to_middle_transfer[0], leaf_coefficient, pre...]
    dot_general x2, matrix products: 10 us -> 8.03 us  [apply_matrix(): jnp.dot(diag_blocks[0], vector, preferred_element_type=jnp.float32)]
    dot_general x2, matrix products: 2.61 us -> 0.63 us  [far_field(): jnp.einsum('kab,kbr->ar', cluster_coupling[0], jnp.take(all_clusters, clu...]
    gather x2, local copies, waits for them, and re-layouts: 3.04 us -> 1.15 us  [far_field(): jnp.take(group_coefs, group_lists[0], axis=0)]
    dot_general x2, matrix products: 4.72 us -> 3.03 us  [far_field(): jnp.dot(bases[0], leaf_grand_total, preferred_element_type=single_precision)]
  transfers between devices with their start and end apart: 2 -> 0, of which waited for: 2 -> 0; matrix products, arithmetic and copies ran while one was open for 8% -> 0% of each run, Pallas kernels for 0% -> 0%
where the time goes in v1:
time: 132 us; the launch traced here: 131 us
  blocking collectives  90.3 us (68%)
  matrix products  26.8 us (20%)
  local copies, waits for them, and re-layouts  9.25 us (7%)
  other arithmetic  4.69 us (4%)
    all_gather x2, blocking collectives, far_field(): lax.all_gather(cluster_half, ('top', 'mid'), axis=0, tiled=True)  44.6 us
    all_gather x2, blocking collectives, far_field(): lax.all_gather(leaf_coefficient, 'leaf', axis=0, tiled=True)  24.5 us
    all_gather x2, blocking collectives, summed_here(): parts = lax.all_gather(array, axis, axis=0, tiled=False)  21.1 us
    dot_general x2, matrix products, smooth(): jnp.dot(precond[0], residual.astype(jnp.bfloat16), preferred_element_type...  8.27 us
    dot_general x2, matrix products, apply_matrix(): jnp.dot(diag_blocks[0], vector, preferred_element_type=jnp.float32)  8.03 us
    dot_general x2, matrix products, far_field(): jnp.dot(bases[0], leaf_grand_total, preferred_element_type=single_precision)  3.03 us
    unnamed x37, local copies, waits for them, and re-layouts  2.74 us

profile of v1, /device:TPU:1, one launch (start us, length us, event | category | flops | bytes accessed | tf_op | source)
XLA Modules:
  0.0 131.4 jit_solution(12813554577486661431)
XLA Ops:
  0.0 0.0 copy-start
  0.0 0.7 compare_and_fusion.1
  0.7 0.7 compare_and_fusion
  1.4 0.7 fusion.91
  2.1 0.7 compare_select_fusion.1
  2.7 0.7 compare_select_fusion
  3.4 1.3 gather_fusion
  4.7 0.7 compare_and_fusion.2
  5.4 0.0 copy-done
  5.4 1.5 %convolution_convert_fusion.1 = bf16[128,256]{1,0:T(8,128)(2,1)S(1)} fusion(bf16[1536,256]{1,0:T(8,128)(2,1)} %param.21, bf16[1,1536,128]{2,1,0:T(8,128)(2,1)S(1)} %copy-done), kind=kOutput, calls=%fused_computation.41 | convolution fusion | flops 100696064 | bytes 1245184 | tf_op jit(solution)/shard_map/na,nr->ar/dot_general | solution.py:31
  6.9 0.0 copy-done.6
  6.9 0.2 fusion.41
  7.1 13.3 %all_gather.24 = bf16[512,256]{1,0:T(8,128)(2,1)S(1)} all-gather(bf16[128,256]{1,0:T(8,128)(2,1)S(1)} %convolution_convert_fusion.1), channel_id=1, replica_groups=mesh['top'=4,'mid'=2,'leaf'=4] {'leaf'}, dimensions={0}, use_global_device_ids=true | all-gather | bytes 327680 | tf_op jit(solution)/shard_map/all_gather | solution.py:40
  20.4 0.6 gather_fusion.1
  20.9 0.0 copy-done.12
  20.9 1.0 convolution_bitcast_fusion.2
  21.9 0.0 copy-done.10
  21.9 10.3 %all-gather = bf16[512,256]{0,1:T(8,128)(2,1)S(1)} all-gather(bf16[128,256]{0,1:T(8,128)(2,1)S(1)} %fusion.41), channel_id=2, replica_groups=mesh['top'=4,'mid'=2,'leaf'=4] {'leaf'}, dimensions={0}, use_global_device_ids=true | all-gather | bytes 327680 | tf_op jit(solution)/shard_map/all_gather | solution.py:10
  32.3 0.1 reshape.129
  32.3 0.3 reduce_sum.42
  32.7 0.0 copy-start.14
  32.7 23.7 %all_gather.27 = bf16[1024,256]{0,1:T(8,128)(2,1)S(1)} all-gather(bf16[128,256]{0,1:T(8,128)(2,1)S(1)} %reduce_sum.42), channel_id=1, replica_groups=mesh['top'=4,'mid'=2,'leaf'=4] {'top','mid'}, dimensions={0}, use_global_device_ids=true | all-gather | bytes 589824 | tf_op jit(solution)/shard_map/all_gather | solution.py:49
  56.4 0.2 copy.39
  56.6 0.6 gather_fusion.2
  57.1 0.0 copy-done.4
  57.2 0.3 bitcast_reduce_fusion.1
  57.5 0.6 gather_fusion.3
  58.1 0.0 copy-done.16
  58.1 0.0 copy-done.14
  58.1 0.3 convolution_bitcast_fusion.6
  58.4 0.0 copy-done.8
  58.4 1.0 fusion.37
  59.4 0.0 copy-done.2
  59.4 1.2 copy.37
  60.6 3.8 %fusion.6 = f32[1536,256]{1,0:T(8,128)S(1)} fusion(bf16[1536,256]{1,0:T(8,128)(2,1)S(1)} %copy-done.2, bf16[1,1536,1536]{2,1,0:T(8,128)(2,1)} %param.22), kind=kOutput, calls=%fused_computation.13 | convolution fusion | flops 1207959552 | bytes 7077888 | tf_op jit(solution)/shard_map/dot_general | solution.py:110
  64.4 1.5 %fusion.33 = bf16[1536,256]{1,0:T(8,128)(2,1)S(1)} fusion(f32[1536,256]{1,0:T(8,128)S(1)} %fusion.6, bf16[1536,256]{1,0:T(8,128)(2,1)S(1)} %copy-done.1, f32[256,128]{1,0:T(8,128)} %convolution_bitcast_fusion.2, bf16[128,256]{0,1:T(8,128)(2,1)} %fusion.37, bf16[1,1536,128]{2,1,0:T(8,128)(2,1)S(1)} %copy-done, bf16[1,128,128]{2,1,0:T(8,128)(2,1)} %param.25), kind=kOutput, calls=%fused_computation.28 | convolution fusion | flops 110690304 | bytes 3768320 | tf_op jit(solution)/shard_map/dot_general | solution.py:88
  65.9 4.0 %fusion.24 = f32[1536,256]{0,1:T(8,128)S(1)} fusion(bf16[1536,256]{1,0:T(8,128)(2,1)S(1)} %fusion.33, bf16[1,1536,1536]{2,1,0:T(8,128)(2,1)} %param.23, bf16[1536,256]{0,1:T(8,128)(2,1)} %copy.37), kind=kOutput, calls=%fused_computation.25 | convolution fusion | flops 1209139200 | bytes 7864320 | tf_op jit(solution)/shard_map/dot_general | solution.py:125
  69.9 1.1 copy-done.3
  71.1 0.4 convolution_convert_fusion
  71.4 0.0 copy-start.11
  71.5 0.0 copy-start.13
  71.5 0.4 copy-done.7
  71.8 0.1 fusion.42
  72.0 10.8 %all-gather.1 = bf16[512,256]{0,1:T(8,128)(2,1)S(1)} all-gather(bf16[128,256]{0,1:T(8,128)(2,1)S(1)} %fusion.42), channel_id=3, replica_groups=mesh['top'=4,'mid'=2,'leaf'=4] {'leaf'}, dimensions={0}, use_global_device_ids=true | all-gather | bytes 327680 | tf_op jit(solution)/shard_map/all_gather | solution.py:10
  82.8 0.1 reshape.130
  82.9 0.3 reduce_sum.44
  83.2 11.2 %all_gather.28 = bf16[512,256]{0,1:T(8,128)(2,1)S(1)} all-gather(bf16[128,256]{0,1:T(8,128)(2,1)S(1)} %bitcast.172), channel_id=1, replica_groups=mesh['top'=4,'mid'=2,'leaf'=4] {'leaf'}, dimensions={0}, use_global_device_ids=true | all-gather | bytes 327680 | tf_op jit(solution)/shard_map/all_gather | solution.py:40
  94.5 0.1 copy.64
  94.6 0.0 copy-start.5
  94.6 0.6 gather_fusion.4
  95.2 0.0 copy-done.11
  95.2 0.0 copy-done.13
  95.2 1.0 convolution_bitcast_fusion.1
  96.2 20.9 %all_gather.31 = bf16[1024,256]{0,1:T(8,128)(2,1)S(1)} all-gather(bf16[128,256]{0,1:T(8,128)(2,1)S(1)} %reduce_sum.44), channel_id=1, replica_groups=mesh['top'=4,'mid'=2,'leaf'=4] {'top','mid'}, dimensions={0}, use_global_device_ids=true | all-gather | bytes 589824 | tf_op jit(solution)/shard_map/all_gather | solution.py:49
  117.1 0.2 copy.46
  117.3 0.6 gather_fusion.5
  117.9 0.3 bitcast_reduce_fusion
  118.3 0.6 gather_fusion.6
  118.9 0.3 convolution_bitcast_fusion.4
  119.2 1.0 fusion.39
  120.2 4.2 %fusion.4 = f32[256,1536]{0,1:T(8,128)S(1)} fusion(bf16[1,1536,1536]{2,1,0:T(8,128)(2,1)} %param.22, f32[1536,256]{0,1:T(8,128)} %copy-done.3), kind=kOutput, calls=%fused_computation.11 | convolution fusion | flops 1208352768 | bytes 7864320 | tf_op jit(solution)/shard_map/dot_general | solution.py:110
  124.4 1.5 %fusion.34 = bf16[1536,256]{1,0:T(8,128)(2,1)S(1)} fusion(f32[256,1536]{0,1:T(8,128)S(1)} %fusion.4, bf16[1536,256]{1,0:T(8,128)(2,1)S(1)} %copy-done.1, f32[256,128]{1,0:T(8,128)} %convolution_bitcast_fusion.1, bf16[128,256]{0,1:T(8,128)(2,1)} %fusion.39, bf16[1,1536,128]{2,1,0:T(8,128)(2,1)S(1)} %copy-done, bf16[1,128,128]{2,1,0:T(8,128)(2,1)} %param.25), kind=kOutput, calls=%fused_computation.29 | convolution fusion | flops 110690304 | bytes 3768320 | tf_op jit(solution)/shard_map/dot_general | solution.py:88
  126.0 4.3 %fusion.30 = bf16[1536,256]{0,1:T(8,128)(2,1)S(1)} fusion(f32[1536,256]{0,1:T(8,128)} %copy-done.3, bf16[1536,256]{1,0:T(8,128)(2,1)S(1)} %fusion.34, bf16[1,1536,1536]{2,1,0:T(8,128)(2,1)} %param.23), kind=kOutput, calls=%fused_computation.27 | convolution fusion | flops 1209139200 | bytes 7864320 | tf_op jit(solution)/shard_map/dot_general | solution.py:125
  130.2 1.2 copy.52
  (22 shorter events, 0.1 us)
Async XLA Ops:
  0.0 5.4 %copy-start = (bf16[1,1536,128]{2,1,0:T(8,128)(2,1)S(1)}, bf16[1,1536,128]{2,1,0:T(8,128)(2,1)}, u32[]{:S(2)}) copy-start(bf16[1,1536,128]{2,1,0:T(8,128)(2,1)} %param.24) | copy-start | bytes 1179652
  0.0 6.9 %copy-start.6 = (bf16[1,128,128]{2,1,0:T(8,128)(2,1)S(1)}, bf16[1,128,128]{2,1,0:T(8,128)(2,1)}, u32[]{:S(2)}) copy-start(bf16[1,128,128]{2,1,0:T(8,128)(2,1)} %param.25) | copy-start | bytes 98308
  0.0 20.9 %copy-start.12 = (bf16[1,4,128,128]{3,2,1,0:T(8,128)(2,1)S(1)}, bf16[1,4,128,128]{3,2,1,0:T(8,128)(2,1)}, u32[]{:S(2)}) copy-start(bf16[1,4,128,128]{3,2,1,0:T(8,128)(2,1)} %param.27) | copy-start | bytes 393220
  0.7 57.4 %copy-start.16 = (pred[3]{0:T(512)(128)(4,1)}, pred[3]{0:T(512)(128)(4,1)S(1)}, u32[]{:S(2)}) copy-start(pred[3]{0:T(512)(128)(4,1)S(1)} %compare_and_fusion.1) | copy-start | bytes 13
  5.4 16.6 %copy-start.10 = (pred[4]{0:T(512)(128)(4,1)}, pred[4]{0:T(512)(128)(4,1)S(1)}, u32[]{:S(2)}) copy-start(pred[4]{0:T(512)(128)(4,1)S(1)} %get-tuple-element.6) | copy-start | bytes 16
  21.9 35.2 %copy-start.4 = (bf16[8,128,128]{2,1,0:T(8,128)(2,1)S(1)}, bf16[8,128,128]{2,1,0:T(8,128)(2,1)}, u32[]{:S(2)}) copy-start(bf16[8,128,128]{2,1,0:T(8,128)(2,1)} %param.26) | copy-start | bytes 786436
  32.7 25.4 %copy-start.14 = (bf16[1,3,128,128]{3,2,1,0:T(8,128)(2,1)S(1)}, bf16[1,3,128,128]{3,2,1,0:T(8,128)(2,1)}, u32[]{:S(2)}) copy-start(bf16[1,3,128,128]{3,2,1,0:T(8,128)(2,1)} %param.28) | copy-start | bytes 294916
  56.4 2.1 %copy-start.8 = (bf16[1,2,128,128]{3,2,1,0:T(8,128)(2,1)S(1)}, bf16[1,2,128,128]{3,2,1,0:T(8,128)(2,1)}, u32[]{:S(2)}) copy-start(bf16[1,2,128,128]{3,2,1,0:T(8,128)(2,1)} %param.29) | copy-start | bytes 196612
  56.4 3.1 %copy-start.2 = (bf16[1536,256]{1,0:T(8,128)(2,1)S(1)}, bf16[1536,256]{1,0:T(8,128)(2,1)}, u32[]{:S(2)}) copy-start(bf16[1536,256]{1,0:T(8,128)(2,1)} %param.21) | copy-start | bytes 2359300
  60.6 3.8 %copy-start.1 = (bf16[1536,256]{1,0:T(8,128)(2,1)S(1)}, bf16[1536,256]{1,0:T(8,128)(2,1)}, u32[]{:S(2)}) copy-start(bf16[1536,256]{1,0:T(8,128)(2,1)} %param.20) | copy-start | bytes 2359300
  69.9 1.1 copy-start.3
  71.1 0.8 copy-start.7
  71.4 23.7 %copy-start.11 = (pred[4]{0:T(512)(128)(4,1)S(1)}, pred[4]{0:T(512)(128)(4,1)}, u32[]{:S(2)}) copy-start(pred[4]{0:T(512)(128)(4,1)} %copy-done.10) | copy-start | bytes 16
  71.5 23.7 %copy-start.13 = (bf16[1,4,128,128]{3,2,1,0:T(8,128)(2,1)S(1)}, bf16[1,4,128,128]{3,2,1,0:T(8,128)(2,1)}, u32[]{:S(2)}) copy-start(bf16[1,4,128,128]{3,2,1,0:T(8,128)(2,1)} %param.27) | copy-start | bytes 393220
  94.6 23.3 %copy-start.5 = (bf16[8,128,128]{2,1,0:T(8,128)(2,1)S(1)}, bf16[8,128,128]{2,1,0:T(8,128)(2,1)}, u32[]{:S(2)}) copy-start(bf16[8,128,128]{2,1,0:T(8,128)(2,1)} %param.26) | copy-start | bytes 786436
  96.2 22.7 %copy-start.15 = (bf16[1,3,128,128]{3,2,1,0:T(8,128)(2,1)S(1)}, bf16[1,3,128,128]{3,2,1,0:T(8,128)(2,1)}, u32[]{:S(2)}) copy-start(bf16[1,3,128,128]{3,2,1,0:T(8,128)(2,1)} %param.28) | copy-start | bytes 294916
  96.2 22.7 %copy-start.17 = (pred[3]{0:T(512)(128)(4,1)S(1)}, pred[3]{0:T(512)(128)(4,1)}, u32[]{:S(2)}) copy-start(pred[3]{0:T(512)(128)(4,1)} %copy-done.16) | copy-start | bytes 13
  117.1 2.1 %copy-start.9 = (bf16[1,2,128,128]{3,2,1,0:T(8,128)(2,1)S(1)}, bf16[1,2,128,128]{3,2,1,0:T(8,128)(2,1)}, u32[]{:S(2)}) copy-start(bf16[1,2,128,128]{3,2,1,0:T(8,128)(2,1)} %param.29) | copy-start | bytes 196612
